TPU v7x, 32 devices: a whole 2x2x4 slice. The times are simulated.
32 devices in a mesh: rep: 4 (over x, core), own: 8 (over z, y).
Axes of the slice: x: 2, y: 2, z: 4, core: 2. Of those that a mesh axis runs over, the one named last changes fastest.
Arguments:
- weights: float32 [4, 256, 8, 2048], P('rep', 'own'), may hold values from -6 to 6
- anchor: float32 [832, 8, 2048], P('own'), may hold values from -6 to 6
- momentum: float32 [832, 8, 2048], P('own'), may hold values from -3 to 3
- owner: int32 [256], replicated, may hold values from 0 to 7, as said below
- emb_weights: float32 [4, 1024, 2048], P('rep', 'own'), may hold values from -6 to 6
- emb_anchor: float32 [1024, 2048], P('own'), may hold values from -6 to 6
- emb_momentum: float32 [1024, 2048], P('own'), may hold values from -3 to 3
- sketch: float32 [64, 2048], replicated, may hold values from -0.125 to 0.125
- inv_root: float32 [64, 64], replicated
Outputs:
- new_weights: float32 [256, 8, 2048], P('own')
- new_momentum: float32 [832, 8, 2048], P('own')
- new_embedding: float32 [1024, 2048], P('own')
- new_emb_momentum: float32 [1024, 2048], P('own')
Inputs may be any that keep to these rules, and one draw needn't show every extreme that they name: Each owner holds at least 8 and at most 104 tiles, and some owner holds exactly 104. Of the 32 tiles of one aligned block, at most 13 have the same owner, and some block reaches 13.
All inputs are finite; a program needn't handle non-finite values.
Results may differ from a plain program's by a relative error of at most 0.0001.
Values sent between devices are 32-bit elements; how exact they have to be, the bound alone decides.
A program may use at most 128 MiB of HBM per device.

v0:
```python
import functools

import jax
import jax.numpy as jnp
from jax import lax
from jax.experimental import pallas as pl
from jax.experimental.pallas import tpu as pltpu
from jax.sharding import PartitionSpec as P

OUTER_RATE = 0.7
OUTER_MOMENTUM = 0.9


def owner_tables(owner, tiles_dev, per_pair, capacity, own_index, own_count):
    tile_count = owner.shape[0]
    tile_ids = jnp.arange(tile_count, dtype=jnp.int32)
    block_of = tile_ids // tiles_dev
    same_owner = owner[:, None] == owner[None, :]
    earlier = tile_ids[None, :] < tile_ids[:, None]
    slot_rank = jnp.sum(same_owner & earlier, axis=1, dtype=jnp.int32)
    pair_rank = jnp.sum(
        same_owner & earlier & (block_of[:, None] == block_of[None, :]), axis=1, dtype=jnp.int32
    )
    local_owner = lax.dynamic_slice_in_dim(owner, own_index * tiles_dev, tiles_dev)
    local_pair = lax.dynamic_slice_in_dim(pair_rank, own_index * tiles_dev, tiles_dev)
    dest_ids = jnp.arange(own_count, dtype=jnp.int32)[:, None, None]
    pair_ids = jnp.arange(per_pair, dtype=jnp.int32)[None, :, None]
    outgoing_match = (local_owner[None, None, :] == dest_ids) & (
        local_pair[None, None, :] == pair_ids
    )
    local_ids = jnp.arange(tiles_dev, dtype=jnp.int32)[None, None, :]
    local_pick = jnp.sum(jnp.where(outgoing_match, local_ids, 0), axis=2).reshape(-1)
    shard_read = local_owner * per_pair + local_pair
    held_here = owner == own_index
    slot_ids = jnp.arange(capacity, dtype=jnp.int32)[:, None]
    holder_match = held_here[None, :] & (slot_rank[None, :] == slot_ids)
    owner_read = jnp.sum(
        jnp.where(holder_match, (block_of * per_pair + pair_rank)[None, :], 0), axis=1
    )
    is_filled = jnp.any(holder_match, axis=1)
    return_match = (
        held_here[None, None, :]
        & (block_of[None, None, :] == dest_ids)
        & (pair_rank[None, None, :] == pair_ids)
    )
    owner_pick = jnp.sum(jnp.where(return_match, slot_rank[None, None, :], 0), axis=2).reshape(-1)
    return (local_pick, shard_read, owner_read, is_filled, owner_pick)


FIXED = 1.0 + OUTER_MOMENTUM
SQUARED = OUTER_MOMENTUM * OUTER_MOMENTUM


def flip(index, bits):
    out, unit = index, 1
    while unit <= bits:
        if bits & unit:
            out = out + unit - 2 * unit * ((index // unit) % 2)
        unit *= 2
    return out


def route_kernel(
    own_count, per_pair, groups,
    local_pick, shard_read, owner_read, filled, owner_pick, weights, anchor, momentum,
    new_weights, new_momentum,
    anchor_part, momentum_part, mine, core_in, chip_out, chip_in, mean, held_out, held_in,
    mean_out, gathered, fresh, anchor_all, momentum_all,
    local_sem, core_send, core_recv, chip_send, chip_recv, held_send, held_recv,
    mean_send, mean_recv, gc_send, gc_recv, gx_send, gx_recv, gf_send, gf_recv,
    fresh_send, fresh_recv, tile_sem, slot_sem,
):
    rep = lax.axis_index("rep")
    own = lax.axis_index("own")
    core_peer, chip_peer, far_peer = flip(rep, 1), flip(rep, 2), flip(rep, 3)
    tiles, part = mean.shape[0], mean.shape[2]
    slots = anchor_part.shape[0]

    def columns(index):
        return pl.ds(pl.multiple_of(index * part, 128), part)

    def to_rep(src, dst, send, recv, peer):
        return pltpu.make_async_remote_copy(
            src_ref=src, dst_ref=dst, send_sem=send, recv_sem=recv,
            device_id=(peer, own), device_id_type=pl.DeviceIdType.MESH,
        )

    def to_own(src, dst, send, recv, peer):
        return pltpu.make_async_remote_copy(
            src_ref=src, dst_ref=dst, send_sem=send, recv_sem=recv,
            device_id=(rep, peer), device_id_type=pl.DeviceIdType.MESH,
        )

    first = [
        pltpu.make_async_copy(anchor.at[:, :, columns(rep)], anchor_part, local_sem.at[0]),
        pltpu.make_async_copy(momentum.at[:, :, columns(rep)], momentum_part, local_sem.at[1]),
        pltpu.make_async_copy(weights.at[0, :, :, columns(rep)], mine.at[0], local_sem.at[2]),
        pltpu.make_async_copy(weights.at[0, :, :, columns(chip_peer)], mine.at[1], local_sem.at[3]),
    ]
    for copy in first:
        copy.start()

    barrier = pltpu.get_barrier_semaphore()
    for peer in (core_peer, chip_peer):
        pl.semaphore_signal(
            barrier, inc=1, device_id=(peer, own), device_id_type=pl.DeviceIdType.MESH
        )
    for k in range(1, own_count):
        pl.semaphore_signal(
            barrier, inc=1, device_id=(rep, flip(own, k)), device_id_type=pl.DeviceIdType.MESH
        )
    pl.semaphore_wait(barrier, own_count + 1)

    core_copies = [
        to_rep(
            weights.at[0, :, :, columns(source)], core_in.at[j], core_send.at[j],
            core_recv.at[j], core_peer,
        )
        for j, source in ((1, far_peer), (0, core_peer))
    ]
    for copy in core_copies:
        copy.start()

    first[0].wait()
    first[1].wait()
    held_copies = []
    for k in list(range(1, own_count)) + [0]:
        peer = flip(own, k)

        def fill(p, carry, k=k, peer=peer):
            slot = owner_pick[peer * per_pair + p]
            a = anchor_part[slot]
            value = a - OUTER_RATE * (FIXED * a + SQUARED * momentum_part[slot])
            if k == 0:
                held_in[own * per_pair + p] = value
            else:
                held_out[k * per_pair + p] = value
            return carry

        lax.fori_loop(0, per_pair, fill, 0)
        if k:
            copy = to_own(
                held_out.at[pl.ds(k * per_pair, per_pair)],
                held_in.at[pl.ds(own * per_pair, per_pair)],
                held_send.at[k], held_recv.at[k], peer,
            )
            copy.start()
            held_copies.append(copy)

    whole = [
        pltpu.make_async_copy(anchor, anchor_all, local_sem.at[4]),
        pltpu.make_async_copy(momentum, momentum_all, local_sem.at[5]),
    ]
    for copy in whole:
        copy.start()

    first[2].wait()
    first[3].wait()
    core_copies[0].wait_recv()

    def half_sum(t, carry):
        chip_out[t] = mine[1, t] + core_in[1, t]
        return carry

    lax.fori_loop(0, tiles, half_sum, 0)
    chip_copy = to_rep(chip_out, chip_in, chip_send.at[0], chip_recv.at[0], chip_peer)
    chip_copy.start()
    core_copies[1].wait_recv()
    chip_copy.wait_recv()

    def full_sum(t, carry):
        mean[t] = (mine[0, t] + core_in[0, t] + chip_in[t]) * 0.25
        return carry

    lax.fori_loop(0, tiles, full_sum, 0)

    mean_copies = {}
    for k in list(range(1, own_count)) + [0]:
        peer = flip(own, k)

        def fill_mean(p, carry, k=k, peer=peer):
            value = mean[local_pick[peer * per_pair + p]]
            if k == 0:
                gathered[rep, own * per_pair + p] = value
            else:
                mean_out[k * per_pair + p] = value
            return carry

        lax.fori_loop(0, per_pair, fill_mean, 0)
        if k:
            copy = to_own(
                mean_out.at[pl.ds(k * per_pair, per_pair)],
                gathered.at[rep, pl.ds(own * per_pair, per_pair)],
                mean_send.at[k], mean_recv.at[k], peer,
            )
            copy.start()
            mean_copies[k] = copy

    near, cross, passed = {}, {}, {}

    def spread(k):
        rows = pl.ds(flip(own, k) * per_pair, per_pair)
        if k:
            mean_copies[k].wait_recv()
        here = gathered.at[rep, rows]
        cross[k] = to_rep(here, here, gx_send.at[k], gx_recv.at[k], chip_peer)
        near[k] = to_rep(here, here, gc_send.at[k], gc_recv.at[k], core_peer)
        cross[k].start()
        near[k].start()

    def pass_on(k):
        rows = pl.ds(flip(own, k) * per_pair, per_pair)
        cross[k].wait_recv()
        there = gathered.at[chip_peer, rows]
        passed[k] = to_rep(there, there, gf_send.at[k], gf_recv.at[k], core_peer)
        passed[k].start()

    early = min(2, own_count)
    for k in range(early):
        spread(k)

    for copy in held_copies:
        copy.wait_recv()

    def renew(t, carry):
        fresh[rep, t] = held_in[shard_read[t]] + (OUTER_RATE * FIXED) * mean[t]
        return carry

    lax.fori_loop(0, tiles, renew, 0)
    fresh_copies = [
        to_rep(fresh.at[rep], fresh.at[rep], fresh_send.at[0], fresh_recv.at[0], chip_peer),
        to_rep(fresh.at[rep], fresh.at[rep], fresh_send.at[1], fresh_recv.at[1], core_peer),
    ]
    for copy in fresh_copies:
        copy.start()

    for k in range(early, own_count):
        spread(k)
        pass_on(k - early)
    fresh_copies[0].wait_recv()
    last = to_rep(
        fresh.at[chip_peer], fresh.at[chip_peer], fresh_send.at[2], fresh_recv.at[2], core_peer
    )
    last.start()
    fresh_copies.append(last)
    for k in range(own_count - early, own_count):
        pass_on(k)

    fresh_copies[1].wait_recv()
    last.wait_recv()
    tile_copies = [
        pltpu.make_async_copy(
            fresh.at[q], new_weights.at[:, :, pl.ds(q * part, part)], tile_sem.at[q]
        )
        for q in range(4)
    ]
    for copy in tile_copies:
        copy.start()
    for copy in whole:
        copy.wait()
    for k in range(own_count):
        near[k].wait_recv()
        passed[k].wait_recv()

    size = slots // groups
    slot_copies = []
    for g in range(groups):

        def advance(j, carry, g=g):
            s = g * size + j
            row = owner_read[s]
            kept = jnp.full((8, 128), filled[s], jnp.int32) > 0
            kept = jnp.concatenate([kept.astype(jnp.float32)] * (part // 128), axis=1) > 0.5
            for q in range(4):
                at = pl.ds(q * part, part)
                moved = OUTER_MOMENTUM * momentum_all[s, :, at] + (
                    anchor_all[s, :, at] - gathered[q, row]
                )
                momentum_all[s, :, at] = jnp.where(kept, moved, 0.0)
            return carry

        lax.fori_loop(0, size, advance, 0)
        copy = pltpu.make_async_copy(
            momentum_all.at[pl.ds(g * size, size)],
            new_momentum.at[pl.ds(g * size, size)],
            slot_sem.at[g],
        )
        copy.start()
        slot_copies.append(copy)

    for copy in core_copies + [chip_copy] + held_copies + fresh_copies:
        copy.wait_send()
    for k in range(own_count):
        if k:
            mean_copies[k].wait_send()
        near[k].wait_send()
        cross[k].wait_send()
        passed[k].wait_send()
    for copy in tile_copies + slot_copies:
        copy.wait()


def route(weights, anchor, momentum, tables, own_count, per_pair):
    tiles, rows, width = weights.shape[1:]
    slots, part = anchor.shape[0], width // 4
    pairs = own_count * per_pair
    groups = 8 if slots % 8 == 0 else 1
    f32, dma = jnp.float32, pltpu.SemaphoreType.DMA
    scratch = [
        pltpu.VMEM((slots, rows, part), f32), pltpu.VMEM((slots, rows, part), f32),
        pltpu.VMEM((2, tiles, rows, part), f32), pltpu.VMEM((2, tiles, rows, part), f32),
        pltpu.VMEM((tiles, rows, part), f32), pltpu.VMEM((tiles, rows, part), f32),
        pltpu.VMEM((tiles, rows, part), f32),
        pltpu.VMEM((pairs, rows, part), f32), pltpu.VMEM((pairs, rows, part), f32),
        pltpu.VMEM((pairs, rows, part), f32), pltpu.VMEM((4, pairs, rows, part), f32),
        pltpu.VMEM((4, tiles, rows, part), f32),
        pltpu.VMEM((slots, rows, width), f32), pltpu.VMEM((slots, rows, width), f32),
        dma((6,)), dma((2,)), dma((2,)), dma((1,)), dma((1,)),
    ] + [dma((own_count,)) for _ in range(10)] + [dma((3,)), dma((3,)), dma((4,)), dma((groups,))]
    return pl.pallas_call(
        functools.partial(route_kernel, own_count, per_pair, groups),
        out_shape=(
            jax.ShapeDtypeStruct((tiles, rows, width), f32),
            jax.ShapeDtypeStruct((slots, rows, width), f32),
        ),
        in_specs=[pl.BlockSpec(memory_space=pltpu.SMEM)] * 5 + [pl.BlockSpec(memory_space=pl.ANY)] * 3,
        out_specs=(pl.BlockSpec(memory_space=pl.ANY), pl.BlockSpec(memory_space=pl.ANY)),
        scratch_shapes=scratch,
        compiler_params=pltpu.CompilerParams(
            collective_id=0, has_side_effects=True, vmem_limit_bytes=60 * 1024 * 1024
        ),
        cost_estimate=pl.CostEstimate(flops=20000000, bytes_accessed=300000000, transcendentals=0),
    )(*tables, weights, anchor, momentum)


def local(
    weights, anchor, momentum, owner, emb_weights, emb_anchor, emb_momentum, sketch, inv_root
):
    own_count = lax.axis_size("own")
    rep_count = lax.axis_size("rep")
    own_index = lax.axis_index("own")
    tiles_dev = weights.shape[1]
    capacity = anchor.shape[0]
    half_tiles = min(tiles_dev // 2, own_count)
    hot_count = max(own_count // 4, 1)
    per_pair = (tiles_dev - half_tiles) // hot_count + 1
    local_pick, shard_read, owner_read, is_filled, owner_pick = owner_tables(
        owner, tiles_dev, per_pair, capacity, own_index, own_count
    )
    tables = (local_pick, shard_read, owner_read, is_filled.astype(jnp.int32), owner_pick)
    new_weights, new_momentum = route(weights, anchor, momentum, tables, own_count, per_pair)
    highest = lax.Precision.HIGHEST
    emb_diff = emb_anchor - emb_weights[0]
    local_sketch = lax.dot_general(
        sketch,
        emb_diff,
        (((1,), (1,)), ((), ())),
        precision=highest,
        preferred_element_type=jnp.float32,
    )
    sketch_mean = lax.psum(local_sketch, "rep") * (1.0 / rep_count)
    basis_rows = jnp.dot(
        inv_root, sketch_mean, precision=highest, preferred_element_type=jnp.float32
    )
    local_factor = jnp.dot(
        basis_rows, emb_diff, precision=highest, preferred_element_type=jnp.float32
    )
    factor = lax.psum(local_factor, ("rep", "own")) * (1.0 / rep_count)
    approx = lax.dot_general(
        basis_rows,
        factor,
        (((0,), (0,)), ((), ())),
        precision=highest,
        preferred_element_type=jnp.float32,
    )
    new_emb_momentum = OUTER_MOMENTUM * emb_momentum + approx
    new_embedding = emb_anchor - OUTER_RATE * (approx + OUTER_MOMENTUM * new_emb_momentum)
    return (new_weights, new_momentum, new_embedding, new_emb_momentum)


def solution(mesh):
    placed = (
        P("rep", "own", None, None),
        P("own", None, None),
        P("own", None, None),
        P(),
        P("rep", "own", None),
        P("own", None),
        P("own", None),
        P(),
        P(),
    )
    return jax.shard_map(
        local,
        mesh=mesh,
        in_specs=placed,
        out_specs=(P("own", None, None), P("own", None, None), P("own", None), P("own", None)),
        check_vma=False,
    )
```

profile of v0, /device:TPU:0, one launch (start us, length us, event | category | flops | bytes accessed | tf_op | source)
XLA Modules:
  0.0 208.4 jit_solution(7785866169701776711)
XLA Ops:
  7.2 0.0 all-reduce.2.cloned.1.call-start
  7.2 1.0 copy-done
  8.2 2.5 %convolution_bitcast_fusion = f32[64,128]{0,1:T(8,128)S(1)} fusion(f32[64,2048]{1,0:T(8,128)S(1)} %copy-done, f32[128,2048]{1,0:T(8,128)} %param.14, f32[1,128,2048]{2,1,0:T(8,128)} %param.13), kind=kOutput, calls=%fused_computation | convolution fusion | flops 201588736 | bytes 2654208 | tf_op jit(solution)/shard_map/dot_general | solution.py:354
  10.7 13.4 %psum.14 = f32[64,128]{0,1:T(8,128)S(1)} all-reduce(f32[64,128]{0,1:T(8,128)S(1)} %convolution_bitcast_fusion), channel_id=1, replica_groups=mesh['rep'=4,'own'=8] {'rep'}, use_global_device_ids=true, to_apply=%region_6.7 | all-reduce | flops 8192 | bytes 65536 | tf_op jit(solution)/shard_map/psum | solution.py:361
  24.1 1.0 fusion.7
  25.2 3.1 %fusion.2 = f32[64,2048]{1,0:T(8,128)} fusion(f32[128,64]{0,1:T(8,128)S(1)} %fusion.7, f32[128,2048]{1,0:T(8,128)} %param.14, f32[1,128,2048]{2,1,0:T(8,128)} %param.13), kind=kOutput, calls=%fused_computation.6 | convolution fusion | flops 201588736 | bytes 2654208 | tf_op jit(solution)/shard_map/dot_general | solution.py:365
  28.2 0.0 all-reduce.2.cloned.1.call-update
  28.3 0.7 broadcast_compare_fusion
  28.9 1.0 convert_reduce_fusion
  30.0 1.3 multiply_add_fusion.2
  31.2 0.3 select_reduce_fusion.2
  31.6 0.1 copy.13
  31.6 0.6 reshape.172.local_pick
  32.3 0.1 fusion.6
  32.4 0.6 convert_element_type.11.filled
  32.9 0.3 select_reduce_fusion
  33.3 0.1 copy.14
  33.3 0.7 reshape.173.owner_pick
  34.0 0.6 select_reduce_fusion.1.owner_read
  34.7 96.2 %shard_map.120 = (f32[32,8,2048]{2,1,0:T(8,128)}, f32[104,8,2048]{2,1,0:T(8,128)}) custom-call(s32[104]{0:T(128)} %reshape.172.local_pick, s32[32]{0:T(128)} %get-tuple-element.12.shard_read, s32[104]{0:T(128)} %select_reduce_fusion.1.owner_read, s32[104]{0:T(128)} %convert_element_type.11.filled, s32[104]{0:T(128)} %reshape.173.owner_pick, ...), custom_call_target="tpu_custom_call" | custom-call | flops 20000000 | bytes 300000000 | tf_op jit(solution)/shard_map/pallas_call | solution.py:320
  130.9 60.9 %all-reduce.2.cloned.1.call-done = f32[64,2048]{1,0:T(8,128)} async-done(((f32[64,2048]{1,0:T(8,128)}), f32[64,2048]{1,0:T(8,128)}) %all-reduce.2.cloned.1.call-update) | async-done | bytes 524304 | tf_op jit(solution)/shard_map/psum | solution.py:368
  191.8 3.7 %multiply_subtract_fusion = (f32[128,2048]{1,0:T(8,128)}, f32[128,2048]{1,0:T(8,128)}) fusion(f32[128,2048]{1,0:T(8,128)S(1)} %copy-done.1, f32[128,2048]{1,0:T(8,128)S(1)} %copy-done.3, f32[128,64]{0,1:T(8,128)S(1)} %fusion.7, f32[64,2048]{1,0:T(8,128)} %all-reduce.2.cloned.1.call-done), kind=kOutput, calls=%fused_computation.2 | convolution fusion | flops 203030528 | bytes 4751360 | tf_op jit(solution)/shard_map/dot_general | solution.py:369
  195.5 3.1 %copy.18 = f32[32,8,2048]{2,1,0:T(8,128)} copy(f32[32,8,2048]{2,1,0:T(8,128)} %get-tuple-element.19) | data formatting | bytes 4194304
  198.6 2.9 %copy.19 = f32[104,8,2048]{2,1,0:T(8,128)} copy(f32[104,8,2048]{2,1,0:T(8,128)S(1)} %copy-done.2) | data formatting | bytes 13631488
  (13 shorter events, 0.1 us)
Async XLA Ops:
  7.2 1.0 copy-start
  7.2 184.6 %all-reduce.2.cloned.1.call-start = ((), (), s32[]{:S(2)}) async-start(), calls=%async_computation | async-start | bytes 1048576 | tf_op jit(solution)/shard_map/psum | solution.py:368
  34.6 157.1 %copy-start.1 = (f32[128,2048]{1,0:T(8,128)S(1)}, f32[128,2048]{1,0:T(8,128)}, u32[]{:S(2)}) copy-start(f32[128,2048]{1,0:T(8,128)} %param.14) | copy-start | bytes 3145732
  34.7 157.1 %copy-start.3 = (f32[128,2048]{1,0:T(8,128)S(1)}, f32[128,2048]{1,0:T(8,128)}, u32[]{:S(2)}) copy-start(f32[128,2048]{1,0:T(8,128)} %param.15) | copy-start | bytes 3145732
  191.8 6.9 %copy-start.2 = (f32[104,8,2048]{2,1,0:T(8,128)S(1)}, f32[104,8,2048]{2,1,0:T(8,128)}, u32[]{:S(2)}) copy-start(f32[104,8,2048]{2,1,0:T(8,128)} %get-tuple-element.20) | copy-start | bytes 20447236
Sparse Core Ops, SparseCore 0:
  28.4 163.3 all-reduce.1
where the time goes:
time: 209 us; the launch traced here: 208 us
  Pallas kernels  96.2 us (46%)
  waiting for transfers between devices  60.9 us (29%)
  between operations  14.1 us (7%)
  blocking collectives  13.4 us (6%)
  matrix products  10.3 us (5%)
  local copies, waits for them, and re-layouts  8.45 us (4%)
  other arithmetic  4.95 us (2%)
    pallas_call x1, Pallas kernels, route(): pl.pallas_call(functools.partial(route_kernel, own_count, per_pair, group...  96.2 us
    psum x1, waiting for transfers between devices, local(): factor = lax.psum(local_factor, ('rep', 'own')) * (1.0 / rep_count)  60.9 us
    psum x1, blocking collectives, local(): sketch_mean = lax.psum(local_sketch, 'rep') * (1.0 / rep_count)  13.4 us
    unnamed x10, local copies, waits for them, and re-layouts  7.02 us
  transfers between devices with their start and end apart: 1, of which 1 were waited for; matrix products, arithmetic and copies ran while one was open for 3% of the time, Pallas kernels for 46%

commit v1 on v0

--- a/solution.py
+++ b/solution.py
@@ -63,12 +63,16 @@
 def route_kernel(
     own_count, per_pair, groups,
     local_pick, shard_read, owner_read, filled, owner_pick, weights, anchor, momentum,
-    new_weights, new_momentum,
+    emb_weights, emb_anchor, sketch, inv_root,
+    new_weights, new_momentum, factor_out, basis_out,
     anchor_part, momentum_part, mine, core_in, chip_out, chip_in, mean, held_out, held_in,
     mean_out, gathered, fresh, anchor_all, momentum_all,
     local_sem, core_send, core_recv, chip_send, chip_recv, held_send, held_recv,
     mean_send, mean_recv, gc_send, gc_recv, gx_send, gx_recv, gf_send, gf_recv,
     fresh_send, fresh_recv, tile_sem, slot_sem,
+    diff, sketch_own, sketch_half, sketch_core, sketch_chip, factor_own, factor_core,
+    factor_half, factor_chip, factor_quarter, factor_in, factor_sum, factor_all,
+    sk_send, sk_recv, fa_send, fa_recv, fr_send, fr_recv, fg_send, fg_recv, factor_sem,
 ):
     rep = lax.axis_index("rep")
     own = lax.axis_index("own")
@@ -120,6 +124,20 @@
     ]
     for copy in core_copies:
         copy.start()
+
+    highest = lax.Precision.HIGHEST
+    f32 = jnp.float32
+    diff[...] = emb_anchor[...] - emb_weights[0]
+    sketched = jnp.zeros(sketch_own.shape, f32)
+    for q in range(4):
+        at = slice(q * part, (q + 1) * part)
+        sketched = sketched + lax.dot_general(
+            sketch[:, at], diff[:, at], (((1,), (1,)), ((), ())),
+            precision=highest, preferred_element_type=f32,
+        )
+    sketch_own[...] = sketched
+    small_copies = [to_rep(sketch_own, sketch_core, sk_send.at[0], sk_recv.at[0], core_peer)]
+    small_copies[0].start()
 
     first[0].wait()
     first[1].wait()
@@ -154,6 +172,12 @@
     for copy in whole:
         copy.start()
 
+    small_copies[0].wait_recv()
+    sketch_half[...] = sketch_own[...] + sketch_core[...]
+    copy = to_rep(sketch_half, sketch_chip, sk_send.at[1], sk_recv.at[1], chip_peer)
+    copy.start()
+    small_copies.append(copy)
+
     first[2].wait()
     first[3].wait()
     core_copies[0].wait_recv()
@@ -165,6 +189,32 @@
     lax.fori_loop(0, tiles, half_sum, 0)
     chip_copy = to_rep(chip_out, chip_in, chip_send.at[0], chip_recv.at[0], chip_peer)
     chip_copy.start()
+
+    small_copies[1].wait_recv()
+    sketch_mean = (sketch_half[...] + sketch_chip[...]) * 0.25
+    basis = jnp.dot(inv_root[...], sketch_mean, precision=highest, preferred_element_type=f32)
+    basis_out[...] = basis
+    chunks, chunk_rows = factor_own.shape[1:3]
+    for q in range(4):
+        value = jnp.dot(
+            basis, diff[:, q * part : (q + 1) * part],
+            precision=highest, preferred_element_type=f32,
+        )
+        for j in range(chunks):
+            factor_own[q, j] = value[j * chunk_rows : (j + 1) * chunk_rows]
+    for j, source in ((1, far_peer), (0, core_peer)):
+        copy = to_rep(
+            factor_own.at[source], factor_core.at[j], fa_send.at[j], fa_recv.at[j], core_peer
+        )
+        copy.start()
+        small_copies.append(copy)
+    small_copies[2].wait_recv()
+    factor_half[...] = factor_own[chip_peer] + factor_core[1]
+    copy = to_rep(factor_half, factor_chip, fa_send.at[2], fa_recv.at[2], chip_peer)
+    copy.start()
+    small_copies.append(copy)
+    small_copies[3].wait_recv()
+
     core_copies[1].wait_recv()
     chip_copy.wait_recv()
 
@@ -173,6 +223,18 @@
         return carry
 
     lax.fori_loop(0, tiles, full_sum, 0)
+
+    small_copies[4].wait_recv()
+    factor_quarter[...] = factor_own[rep] + factor_core[0] + factor_chip[...]
+    factor_in[own] = factor_quarter[own % chunks]
+    part_copies = []
+    for k in range(1, own_count):
+        peer = flip(own, k)
+        copy = to_own(
+            factor_quarter.at[peer % chunks], factor_in.at[own], fr_send.at[k], fr_recv.at[k], peer
+        )
+        copy.start()
+        part_copies.append(copy)
 
     mean_copies = {}
     for k in list(range(1, own_count)) + [0]:
@@ -234,6 +296,21 @@
     for copy in fresh_copies:
         copy.start()
 
+    for copy in part_copies:
+        copy.wait_recv()
+    total = factor_in[0]
+    for k in range(1, own_count):
+        total = total + factor_in[k]
+    factor_sum[...] = total * 0.25
+    factor_all[rep, own % chunks] = total * 0.25
+    group_copies = []
+    for k in range(1, chunks):
+        copy = to_own(
+            factor_sum, factor_all.at[rep, own % chunks], fg_send.at[k], fg_recv.at[k], flip(own, k)
+        )
+        copy.start()
+        group_copies.append(copy)
+
     for k in range(early, own_count):
         spread(k)
         pass_on(k - early)
@@ -246,6 +323,13 @@
     for k in range(own_count - early, own_count):
         pass_on(k)
 
+    for copy in group_copies:
+        copy.wait_recv()
+    for j, peer in ((3, chip_peer), (4, core_peer)):
+        copy = to_rep(factor_all.at[rep], factor_all.at[rep], fa_send.at[j], fa_recv.at[j], peer)
+        copy.start()
+        small_copies.append(copy)
+
     fresh_copies[1].wait_recv()
     last.wait_recv()
     tile_copies = [
@@ -261,6 +345,13 @@
     for k in range(own_count):
         near[k].wait_recv()
         passed[k].wait_recv()
+
+    small_copies[5].wait_recv()
+    copy = to_rep(
+        factor_all.at[chip_peer], factor_all.at[chip_peer], fa_send.at[5], fa_recv.at[5], core_peer
+    )
+    copy.start()
+    small_copies.append(copy)
 
     size = slots // groups
     slot_copies = []
@@ -288,7 +379,17 @@
         copy.start()
         slot_copies.append(copy)
 
-    for copy in core_copies + [chip_copy] + held_copies + fresh_copies:
+    small_copies[6].wait_recv()
+    small_copies[7].wait_recv()
+    for q in range(4):
+        copy = pltpu.make_async_copy(
+            factor_all.at[q], factor_out.at[:, :, pl.ds(q * part, part)], factor_sem.at[q]
+        )
+        copy.start()
+        tile_copies.append(copy)
+    for copy in core_copies + [chip_copy] + held_copies + fresh_copies + small_copies:
+        copy.wait_send()
+    for copy in part_copies + group_copies:
         copy.wait_send()
     for k in range(own_count):
         if k:
@@ -300,7 +401,7 @@
         copy.wait()
 
 
-def route(weights, anchor, momentum, tables, own_count, per_pair):
+def route(weights, anchor, momentum, embed, tables, own_count, per_pair):
     tiles, rows, width = weights.shape[1:]
     slots, part = anchor.shape[0], width // 4
     pairs = own_count * per_pair
@@ -317,27 +418,42 @@
         pltpu.VMEM((slots, rows, width), f32), pltpu.VMEM((slots, rows, width), f32),
         dma((6,)), dma((2,)), dma((2,)), dma((1,)), dma((1,)),
     ] + [dma((own_count,)) for _ in range(10)] + [dma((3,)), dma((3,)), dma((4,)), dma((groups,))]
+    emb_rows, rank, chunks = embed[1].shape[0], embed[2].shape[0], 8
+    chunk = (rank // chunks, part)
+    scratch += [
+        pltpu.VMEM((emb_rows, width), f32),
+        pltpu.VMEM((rank, emb_rows), f32), pltpu.VMEM((rank, emb_rows), f32),
+        pltpu.VMEM((rank, emb_rows), f32), pltpu.VMEM((rank, emb_rows), f32),
+        pltpu.VMEM((4, chunks) + chunk, f32), pltpu.VMEM((2, chunks) + chunk, f32),
+        pltpu.VMEM((chunks,) + chunk, f32), pltpu.VMEM((chunks,) + chunk, f32),
+        pltpu.VMEM((chunks,) + chunk, f32), pltpu.VMEM((own_count,) + chunk, f32),
+        pltpu.VMEM(chunk, f32), pltpu.VMEM((4, chunks) + chunk, f32),
+        dma((2,)), dma((2,)), dma((6,)), dma((6,)), dma((own_count,)), dma((own_count,)),
+        dma((chunks,)), dma((chunks,)), dma((4,)),
+    ]
     return pl.pallas_call(
         functools.partial(route_kernel, own_count, per_pair, groups),
         out_shape=(
             jax.ShapeDtypeStruct((tiles, rows, width), f32),
             jax.ShapeDtypeStruct((slots, rows, width), f32),
+            jax.ShapeDtypeStruct((chunks, rank // chunks, width), f32),
+            jax.ShapeDtypeStruct((rank, emb_rows), f32),
         ),
-        in_specs=[pl.BlockSpec(memory_space=pltpu.SMEM)] * 5 + [pl.BlockSpec(memory_space=pl.ANY)] * 3,
-        out_specs=(pl.BlockSpec(memory_space=pl.ANY), pl.BlockSpec(memory_space=pl.ANY)),
+        in_specs=[pl.BlockSpec(memory_space=pltpu.SMEM)] * 5 + [pl.BlockSpec(memory_space=pl.ANY)] * 3
+        + [pl.BlockSpec(memory_space=pltpu.VMEM)] * 4,
+        out_specs=(pl.BlockSpec(memory_space=pl.ANY),) * 3 + (pl.BlockSpec(memory_space=pltpu.VMEM),),
         scratch_shapes=scratch,
         compiler_params=pltpu.CompilerParams(
             collective_id=0, has_side_effects=True, vmem_limit_bytes=60 * 1024 * 1024
         ),
         cost_estimate=pl.CostEstimate(flops=20000000, bytes_accessed=300000000, transcendentals=0),
-    )(*tables, weights, anchor, momentum)
+    )(*tables, weights, anchor, momentum, *embed)
 
 
 def local(
     weights, anchor, momentum, owner, emb_weights, emb_anchor, emb_momentum, sketch, inv_root
 ):
     own_count = lax.axis_size("own")
-    rep_count = lax.axis_size("rep")
     own_index = lax.axis_index("own")
     tiles_dev = weights.shape[1]
     capacity = anchor.shape[0]
@@ -348,24 +464,12 @@
         owner, tiles_dev, per_pair, capacity, own_index, own_count
     )
     tables = (local_pick, shard_read, owner_read, is_filled.astype(jnp.int32), owner_pick)
-    new_weights, new_momentum = route(weights, anchor, momentum, tables, own_count, per_pair)
+    embed = (emb_weights, emb_anchor, sketch, inv_root)
+    new_weights, new_momentum, factor, basis_rows = route(
+        weights, anchor, momentum, embed, tables, own_count, per_pair
+    )
+    factor = factor.reshape(sketch.shape)
     highest = lax.Precision.HIGHEST
-    emb_diff = emb_anchor - emb_weights[0]
-    local_sketch = lax.dot_general(
-        sketch,
-        emb_diff,
-        (((1,), (1,)), ((), ())),
-        precision=highest,
-        preferred_element_type=jnp.float32,
-    )
-    sketch_mean = lax.psum(local_sketch, "rep") * (1.0 / rep_count)
-    basis_rows = jnp.dot(
-        inv_root, sketch_mean, precision=highest, preferred_element_type=jnp.float32
-    )
-    local_factor = jnp.dot(
-        basis_rows, emb_diff, precision=highest, preferred_element_type=jnp.float32
-    )
-    factor = lax.psum(local_factor, ("rep", "own")) * (1.0 / rep_count)
     approx = lax.dot_general(
         basis_rows,
         factor,

time: 209 us -> 122 us (0.58)
  waiting for transfers between devices: 60.9 us -> 0 us
  between operations: 14.1 us -> 0.69 us
  blocking collectives: 13.4 us -> 0 us
  Pallas kernels: 96.2 us -> 105 us
  matrix products: 10.3 us -> 3.72 us
    psum x1 -> x0, waiting for transfers between devices: 60.9 us -> none  [local(): factor = lax.psum(local_factor, ('rep', 'own')) * (1.0 / rep_count)]
    psum x1 -> x0, blocking collectives: 13.4 us -> none  [local(): sketch_mean = lax.psum(local_sketch, 'rep') * (1.0 / rep_count)]
    pallas_call x1, Pallas kernels: 96.2 us -> 105 us  [route(): pl.pallas_call(functools.partial(route_kernel, own_count, per_pair, group...]
    dot_general x3 -> x0, matrix products: 6.57 us -> none  [the longest x1 3.06 us: local(): jnp.dot(basis_rows, emb_diff, precision=highest, preferred_element_type=j...]
    unnamed x10 -> x8, local copies, waits for them, and re-layouts: 7.02 us -> 6.02 us
  transfers between devices with their start and end apart: 1 -> 0, of which waited for: 1 -> 0; matrix products, arithmetic and copies ran while one was open for 3% -> 0% of each run, Pallas kernels for 46% -> 0%
where the time goes in v1:
time: 122 us
  Pallas kernels  105 us (86%)
  local copies, waits for them, and re-layouts  7.45 us (6%)
  other arithmetic  4.89 us (4%)
  matrix products  3.72 us (3%)
    pallas_call x1, Pallas kernels, route(): pl.pallas_call(functools.partial(route_kernel, own_count, per_pair, group...  105 us
    unnamed x8, local copies, waits for them, and re-layouts  6.02 us
    dot_general x1, matrix products, local(): lax.dot_general(basis_rows, factor, (((0,), (0,)), ((), ())), precision=h...  3.72 us

profile of v1, /device:TPU:0, one launch (start us, length us, event | category | flops | bytes accessed | tf_op | source)
XLA Modules:
  0.0 121.9 jit_solution(15518914510897195890)
XLA Ops:
  0.6 1.0 convert_reduce_fusion
  1.6 1.3 %multiply_add_fusion.2 = (s32[32]{0:T(128)}, s32[32]{0:T(128)S(1)}, s32[32]{0:T(128)S(1)}) fusion(s32[256]{0:T(256)} %param.12, s32[]{:T(128)S(6)} %select_n.40, s32[256]{0:T(256)S(1)} %get-tuple-element.13), kind=kLoop, calls=%fused_computation.25 | loop fusion | flops 64 | bytes 644 | tf_op jit(solution)/shard_map/add | solution.py:33
  2.9 0.3 select_reduce_fusion.2
  3.3 0.1 copy.13
  3.3 0.6 reshape.175.local_pick
  3.9 0.7 broadcast_compare_fusion
  4.6 0.6 select_reduce_fusion.1.owner_read
  5.3 0.1 fusion.4
  5.4 0.5 convert_element_type.11.filled
  5.9 0.3 select_reduce_fusion
  6.2 0.1 copy.14
  6.3 0.7 reshape.176.owner_pick
  7.0 0.0 copy-start.1
  7.0 0.0 copy-start.2
  7.0 105.2 %shard_map.120 = (f32[32,8,2048]{2,1,0:T(8,128)}, f32[104,8,2048]{2,1,0:T(8,128)}, f32[8,8,2048]{2,1,0:T(8,128)}, f32[64,128]{1,0:T(8,128)}) custom-call(s32[104]{0:T(128)} %reshape.175.local_pick, s32[32]{0:T(128)} %get-tuple-element.16.shard_read, s32[104]{0:T(128)} %select_reduce_fusion.1.owner_read, s32[104]{0:T(128)} %convert_element_type.11.filled, ...), custom_call_target="tpu_custom_call" | custom-call | flops 20000000 | bytes 300000000 | tf_op jit(solution)/shard_map/pallas_call | solution.py:434
  112.1 0.0 copy-start
  112.2 0.0 copy-done.1
  112.2 0.0 copy-done.2
  112.2 3.7 %multiply_subtract_fusion = (f32[128,2048]{1,0:T(8,128)}, f32[128,2048]{1,0:T(8,128)}) fusion(f32[128,2048]{1,0:T(8,128)S(1)} %copy-done.1, f32[128,2048]{1,0:T(8,128)S(1)} %copy-done.2, f32[64,128]{1,0:T(8,128)} %get-tuple-element.10, f32[8,8,2048]{2,1,0:T(8,128)} %get-tuple-element.11), kind=kOutput, calls=%fused_computation | convolution fusion | flops 202899456 | bytes 4751360 | tf_op jit(solution)/shard_map/dot_general | solution.py:473
  115.9 3.1 %copy.17 = f32[32,8,2048]{2,1,0:T(8,128)} copy(f32[32,8,2048]{2,1,0:T(8,128)} %get-tuple-element.23) | data formatting | bytes 4194304
  119.0 0.0 copy-done
  119.0 2.9 %copy.18 = f32[104,8,2048]{2,1,0:T(8,128)} copy(f32[104,8,2048]{2,1,0:T(8,128)S(1)} %copy-done) | data formatting | bytes 13631488
  (6 shorter events, 0.0 us)
Async XLA Ops:
  7.0 105.2 %copy-start.1 = (f32[128,2048]{1,0:T(8,128)S(1)}, f32[128,2048]{1,0:T(8,128)}, u32[]{:S(2)}) copy-start(f32[128,2048]{1,0:T(8,128)} %emb_anchor.1) | copy-start | bytes 3145732
  7.0 105.2 %copy-start.2 = (f32[128,2048]{1,0:T(8,128)S(1)}, f32[128,2048]{1,0:T(8,128)}, u32[]{:S(2)}) copy-start(f32[128,2048]{1,0:T(8,128)} %param.15) | copy-start | bytes 3145732
  112.1 6.9 %copy-start = (f32[104,8,2048]{2,1,0:T(8,128)S(1)}, f32[104,8,2048]{2,1,0:T(8,128)}, u32[]{:S(2)}) copy-start(f32[104,8,2048]{2,1,0:T(8,128)} %get-tuple-element.24) | copy-start | bytes 20447236

commit v2 on v1

--- a/solution.py
+++ b/solution.py
@@ -21,30 +21,22 @@
     pair_rank = jnp.sum(
         same_owner & earlier & (block_of[:, None] == block_of[None, :]), axis=1, dtype=jnp.int32
     )
-    local_owner = lax.dynamic_slice_in_dim(owner, own_index * tiles_dev, tiles_dev)
-    local_pair = lax.dynamic_slice_in_dim(pair_rank, own_index * tiles_dev, tiles_dev)
-    dest_ids = jnp.arange(own_count, dtype=jnp.int32)[:, None, None]
-    pair_ids = jnp.arange(per_pair, dtype=jnp.int32)[None, :, None]
-    outgoing_match = (local_owner[None, None, :] == dest_ids) & (
-        local_pair[None, None, :] == pair_ids
-    )
-    local_ids = jnp.arange(tiles_dev, dtype=jnp.int32)[None, None, :]
-    local_pick = jnp.sum(jnp.where(outgoing_match, local_ids, 0), axis=2).reshape(-1)
-    shard_read = local_owner * per_pair + local_pair
+    pair_key = owner * per_pair + pair_rank
+    back_key = block_of * per_pair + pair_rank
     held_here = owner == own_index
+    local_key = jnp.where(block_of == own_index, pair_key, -1)
+    held_key = jnp.where(held_here, back_key, -1)
+    slot_key = jnp.where(held_here, slot_rank, -1)
+    pair_ids = jnp.arange(own_count * per_pair, dtype=jnp.int32)[:, None]
     slot_ids = jnp.arange(capacity, dtype=jnp.int32)[:, None]
-    holder_match = held_here[None, :] & (slot_rank[None, :] == slot_ids)
-    owner_read = jnp.sum(
-        jnp.where(holder_match, (block_of * per_pair + pair_rank)[None, :], 0), axis=1
-    )
-    is_filled = jnp.any(holder_match, axis=1)
-    return_match = (
-        held_here[None, None, :]
-        & (block_of[None, None, :] == dest_ids)
-        & (pair_rank[None, None, :] == pair_ids)
-    )
-    owner_pick = jnp.sum(jnp.where(return_match, slot_rank[None, None, :], 0), axis=2).reshape(-1)
-    return (local_pick, shard_read, owner_read, is_filled, owner_pick)
+
+    def look_up(ids, key, value):
+        return jnp.sum(jnp.where(key[None, :] == ids, value[None, :], 0), axis=1, dtype=jnp.int32)
+
+    local_pick = look_up(pair_ids, local_key, tile_ids - own_index * tiles_dev)
+    owner_pick = look_up(pair_ids, held_key, slot_rank)
+    owner_read = look_up(slot_ids, slot_key, back_key + 1)
+    return (local_pick, pair_key, owner_read, owner_pick)
 
 
 FIXED = 1.0 + OUTER_MOMENTUM
@@ -62,7 +54,7 @@
 
 def route_kernel(
     own_count, per_pair, groups,
-    local_pick, shard_read, owner_read, filled, owner_pick, weights, anchor, momentum,
+    local_pick, pair_key, owner_read, owner_pick, weights, anchor, momentum,
     emb_weights, emb_anchor, sketch, inv_root,
     new_weights, new_momentum, factor_out, basis_out,
     anchor_part, momentum_part, mine, core_in, chip_out, chip_in, mean, held_out, held_in,
@@ -125,6 +117,32 @@
     for copy in core_copies:
         copy.start()
 
+    first[0].wait()
+    first[1].wait()
+    held_copies = []
+    for k in list(range(1, own_count)) + [0]:
+        peer = flip(own, k)
+
+        def fill(p, carry, k=k, peer=peer):
+            slot = owner_pick[peer * per_pair + p]
+            a = anchor_part[slot]
+            value = a - OUTER_RATE * (FIXED * a + SQUARED * momentum_part[slot])
+            if k == 0:
+                held_in[own * per_pair + p] = value
+            else:
+                held_out[k * per_pair + p] = value
+            return carry
+
+        lax.fori_loop(0, per_pair, fill, 0)
+        if k:
+            copy = to_own(
+                held_out.at[pl.ds(k * per_pair, per_pair)],
+                held_in.at[pl.ds(own * per_pair, per_pair)],
+                held_send.at[k], held_recv.at[k], peer,
+            )
+            copy.start()
+            held_copies.append(copy)
+
     highest = lax.Precision.HIGHEST
     f32 = jnp.float32
     diff[...] = emb_anchor[...] - emb_weights[0]
@@ -139,32 +157,6 @@
     small_copies = [to_rep(sketch_own, sketch_core, sk_send.at[0], sk_recv.at[0], core_peer)]
     small_copies[0].start()
 
-    first[0].wait()
-    first[1].wait()
-    held_copies = []
-    for k in list(range(1, own_count)) + [0]:
-        peer = flip(own, k)
-
-        def fill(p, carry, k=k, peer=peer):
-            slot = owner_pick[peer * per_pair + p]
-            a = anchor_part[slot]
-            value = a - OUTER_RATE * (FIXED * a + SQUARED * momentum_part[slot])
-            if k == 0:
-                held_in[own * per_pair + p] = value
-            else:
-                held_out[k * per_pair + p] = value
-            return carry
-
-        lax.fori_loop(0, per_pair, fill, 0)
-        if k:
-            copy = to_own(
-                held_out.at[pl.ds(k * per_pair, per_pair)],
-                held_in.at[pl.ds(own * per_pair, per_pair)],
-                held_send.at[k], held_recv.at[k], peer,
-            )
-            copy.start()
-            held_copies.append(copy)
-
     whole = [
         pltpu.make_async_copy(anchor, anchor_all, local_sem.at[4]),
         pltpu.make_async_copy(momentum, momentum_all, local_sem.at[5]),
@@ -285,7 +277,7 @@
         copy.wait_recv()
 
     def renew(t, carry):
-        fresh[rep, t] = held_in[shard_read[t]] + (OUTER_RATE * FIXED) * mean[t]
+        fresh[rep, t] = held_in[pair_key[own * tiles + t]] + (OUTER_RATE * FIXED) * mean[t]
         return carry
 
     lax.fori_loop(0, tiles, renew, 0)
@@ -359,9 +351,9 @@
 
         def advance(j, carry, g=g):
             s = g * size + j
-            row = owner_read[s]
-            kept = jnp.full((8, 128), filled[s], jnp.int32) > 0
-            kept = jnp.concatenate([kept.astype(jnp.float32)] * (part // 128), axis=1) > 0.5
+            found = owner_read[s]
+            row = jnp.maximum(found - 1, 0)
+            kept = jnp.full((momentum_all.shape[1], part), found, jnp.int32) > 0
             for q in range(4):
                 at = pl.ds(q * part, part)
                 moved = OUTER_MOMENTUM * momentum_all[s, :, at] + (
@@ -439,7 +431,7 @@
             jax.ShapeDtypeStruct((chunks, rank // chunks, width), f32),
             jax.ShapeDtypeStruct((rank, emb_rows), f32),
         ),
-        in_specs=[pl.BlockSpec(memory_space=pltpu.SMEM)] * 5 + [pl.BlockSpec(memory_space=pl.ANY)] * 3
+        in_specs=[pl.BlockSpec(memory_space=pltpu.SMEM)] * 4 + [pl.BlockSpec(memory_space=pl.ANY)] * 3
         + [pl.BlockSpec(memory_space=pltpu.VMEM)] * 4,
         out_specs=(pl.BlockSpec(memory_space=pl.ANY),) * 3 + (pl.BlockSpec(memory_space=pltpu.VMEM),),
         scratch_shapes=scratch,
@@ -460,10 +452,7 @@
     half_tiles = min(tiles_dev // 2, own_count)
     hot_count = max(own_count // 4, 1)
     per_pair = (tiles_dev - half_tiles) // hot_count + 1
-    local_pick, shard_read, owner_read, is_filled, owner_pick = owner_tables(
-        owner, tiles_dev, per_pair, capacity, own_index, own_count
-    )
-    tables = (local_pick, shard_read, owner_read, is_filled.astype(jnp.int32), owner_pick)
+    tables = owner_tables(owner, tiles_dev, per_pair, capacity, own_index, own_count)
     embed = (emb_weights, emb_anchor, sketch, inv_root)
     new_weights, new_momentum, factor, basis_rows = route(
         weights, anchor, momentum, embed, tables, own_count, per_pair

time: 122 us -> 118 us (0.967)
  local copies, waits for them, and re-layouts: 7.45 us -> 6.02 us
  other arithmetic: 4.89 us -> 3.52 us
    add x2 -> x0, other arithmetic: 1.28 us -> none  [the longest x1 1.27 us: owner_tables(): shard_read = local_owner * per_pair + local_pair]
    reshape x2 -> x0, local copies, waits for them, and re-layouts: 1.26 us -> none  [the longest x1 0.67 us: owner_tables(): jnp.sum(jnp.where(return_match, slot_rank[None, None, :], 0), axis=2)]
    select_n x0 -> x1, other arithmetic: none -> 1.25 us  [owner_tables(): local_key = jnp.where(block_of == own_index, pair_key, -1)]
where the time goes in v2:
time: 118 us
  Pallas kernels  104 us (88%)
  local copies, waits for them, and re-layouts  6.02 us (5%)
  matrix products  3.72 us (3%)
  other arithmetic  3.52 us (3%)
    pallas_call x1, Pallas kernels, route(): pl.pallas_call(functools.partial(route_kernel, own_count, per_pair, group...  104 us
    unnamed x8, local copies, waits for them, and re-layouts  6.02 us
    dot_general x1, matrix products, local(): lax.dot_general(basis_rows, factor, (((0,), (0,)), ((), ())), precision=h...  3.72 us

profile of v2, /device:TPU:0, one launch (start us, length us, event | category | flops | bytes accessed | tf_op | source)
XLA Modules:
  0.0 118.3 jit_solution(13127050398095183519)
XLA Ops:
  0.7 1.0 convert_reduce_fusion
  1.7 1.2 %compare_select_fusion = (s32[256]{0:T(256)S(1)}, s32[256]{0:T(256)}, s32[256]{0:T(256)S(1)}, s32[256]{0:T(256)S(1)}, s32[256]{0:T(256)S(1)}) fusion(s32[]{:T(128)S(6)} %axis_index.12, s32[256]{0:T(256)S(1)} %get-tuple-element.13, s32[256]{0:T(256)} %param.12, s32[256]{0:T(256)S(1)} %get-tuple-element.12), kind=kLoop, calls=%fused_computation.17 | loop fusion | flops 4608 | bytes 8196 | tf_op jit(solution)/shard_map/jit(_where)/select_n | solution.py:27
  2.9 0.6 select_reduce_fusion.2.local_pick
  3.5 0.6 select_reduce_fusion
  4.2 0.0 copy-start.1
  4.2 0.0 copy-start.2
  4.2 104.3 %shard_map.120 = (f32[32,8,2048]{2,1,0:T(8,128)}, f32[104,8,2048]{2,1,0:T(8,128)}, f32[8,8,2048]{2,1,0:T(8,128)}, f32[64,128]{1,0:T(8,128)}) custom-call(s32[104]{0:T(128)} %select_reduce_fusion.2.local_pick, s32[256]{0:T(256)} %get-tuple-element.17.pair_key, s32[104]{0:T(128)} %get-tuple-element.22.owner_read, s32[104]{0:T(128)} %get-tuple-element.21.owner_pick, ...), custom_call_target="tpu_custom_call" | custom-call | flops 20000000 | bytes 300000000 | tf_op jit(solution)/shard_map/pallas_call | solution.py:426
  108.5 0.0 copy-start
  108.5 0.0 copy-done.1
  108.5 0.0 copy-done.2
  108.6 3.7 %multiply_subtract_fusion = (f32[128,2048]{1,0:T(8,128)}, f32[128,2048]{1,0:T(8,128)}) fusion(f32[128,2048]{1,0:T(8,128)S(1)} %copy-done.1, f32[128,2048]{1,0:T(8,128)S(1)} %copy-done.2, f32[64,128]{1,0:T(8,128)} %get-tuple-element.10, f32[8,8,2048]{2,1,0:T(8,128)} %get-tuple-element.11), kind=kOutput, calls=%fused_computation | convolution fusion | flops 202899456 | bytes 4751360 | tf_op jit(solution)/shard_map/dot_general | solution.py:462
  112.3 3.1 %copy.15 = f32[32,8,2048]{2,1,0:T(8,128)} copy(f32[32,8,2048]{2,1,0:T(8,128)} %get-tuple-element.27) | data formatting | bytes 4194304
  115.4 0.0 copy-done
  115.4 2.9 %copy.16 = f32[104,8,2048]{2,1,0:T(8,128)} copy(f32[104,8,2048]{2,1,0:T(8,128)S(1)} %copy-done) | data formatting | bytes 13631488
  (2 shorter events, 0.0 us)
Async XLA Ops:
  4.2 104.4 %copy-start.1 = (f32[128,2048]{1,0:T(8,128)S(1)}, f32[128,2048]{1,0:T(8,128)}, u32[]{:S(2)}) copy-start(f32[128,2048]{1,0:T(8,128)} %emb_anchor.1) | copy-start | bytes 3145732
  4.2 104.4 %copy-start.2 = (f32[128,2048]{1,0:T(8,128)S(1)}, f32[128,2048]{1,0:T(8,128)}, u32[]{:S(2)}) copy-start(f32[128,2048]{1,0:T(8,128)} %param.15) | copy-start | bytes 3145732
  108.5 6.9 %copy-start = (f32[104,8,2048]{2,1,0:T(8,128)S(1)}, f32[104,8,2048]{2,1,0:T(8,128)}, u32[]{:S(2)}) copy-start(f32[104,8,2048]{2,1,0:T(8,128)} %get-tuple-element.28) | copy-start | bytes 20447236

commit v3 on v2

--- a/solution.py
+++ b/solution.py
@@ -269,7 +269,7 @@
         passed[k] = to_rep(there, there, gf_send.at[k], gf_recv.at[k], core_peer)
         passed[k].start()
 
-    early = min(2, own_count)
+    early = min(4, own_count)
     for k in range(early):
         spread(k)
 

time: 118 us -> 118 us (level)
  no operation moved by 1% of the time
where the time goes in v3:
time: 118 us
  Pallas kernels  104 us (88%)
  local copies, waits for them, and re-layouts  6.02 us (5%)
  matrix products  3.72 us (3%)
  other arithmetic  3.52 us (3%)
    pallas_call x1, Pallas kernels, route(): pl.pallas_call(functools.partial(route_kernel, own_count, per_pair, group...  104 us
    unnamed x8, local copies, waits for them, and re-layouts  6.02 us
    dot_general x1, matrix products, local(): lax.dot_general(basis_rows, factor, (((0,), (0,)), ((), ())), precision=h...  3.72 us

profile of v3, /device:TPU:0, one launch (start us, length us, event | category | flops | bytes accessed | tf_op | source)
XLA Modules:
  0.0 118.3 jit_solution(10472523559606858337)
XLA Ops:
  0.7 1.0 convert_reduce_fusion
  1.7 1.2 %compare_select_fusion = (s32[256]{0:T(256)S(1)}, s32[256]{0:T(256)}, s32[256]{0:T(256)S(1)}, s32[256]{0:T(256)S(1)}, s32[256]{0:T(256)S(1)}) fusion(s32[]{:T(128)S(6)} %axis_index.12, s32[256]{0:T(256)S(1)} %get-tuple-element.13, s32[256]{0:T(256)} %param.12, s32[256]{0:T(256)S(1)} %get-tuple-element.12), kind=kLoop, calls=%fused_computation.17 | loop fusion | flops 4608 | bytes 8196 | tf_op jit(solution)/shard_map/jit(_where)/select_n | solution.py:27
  2.9 0.6 select_reduce_fusion.2.local_pick
  3.5 0.6 select_reduce_fusion
  4.2 0.0 copy-start.1
  4.2 0.0 copy-start.2
  4.2 104.3 %shard_map.120 = (f32[32,8,2048]{2,1,0:T(8,128)}, f32[104,8,2048]{2,1,0:T(8,128)}, f32[8,8,2048]{2,1,0:T(8,128)}, f32[64,128]{1,0:T(8,128)}) custom-call(s32[104]{0:T(128)} %select_reduce_fusion.2.local_pick, s32[256]{0:T(256)} %get-tuple-element.17.pair_key, s32[104]{0:T(128)} %get-tuple-element.22.owner_read, s32[104]{0:T(128)} %get-tuple-element.21.owner_pick, ...), custom_call_target="tpu_custom_call" | custom-call | flops 20000000 | bytes 300000000 | tf_op jit(solution)/shard_map/pallas_call | solution.py:426
  108.5 0.0 copy-start
  108.5 0.0 copy-done.1
  108.5 0.0 copy-done.2
  108.6 3.7 %multiply_subtract_fusion = (f32[128,2048]{1,0:T(8,128)}, f32[128,2048]{1,0:T(8,128)}) fusion(f32[128,2048]{1,0:T(8,128)S(1)} %copy-done.1, f32[128,2048]{1,0:T(8,128)S(1)} %copy-done.2, f32[64,128]{1,0:T(8,128)} %get-tuple-element.10, f32[8,8,2048]{2,1,0:T(8,128)} %get-tuple-element.11), kind=kOutput, calls=%fused_computation | convolution fusion | flops 202899456 | bytes 4751360 | tf_op jit(solution)/shard_map/dot_general | solution.py:462
  112.3 3.1 %copy.15 = f32[32,8,2048]{2,1,0:T(8,128)} copy(f32[32,8,2048]{2,1,0:T(8,128)} %get-tuple-element.27) | data formatting | bytes 4194304
  115.4 0.0 copy-done
  115.4 2.9 %copy.16 = f32[104,8,2048]{2,1,0:T(8,128)} copy(f32[104,8,2048]{2,1,0:T(8,128)S(1)} %copy-done) | data formatting | bytes 13631488
  (2 shorter events, 0.0 us)
Async XLA Ops:
  4.2 104.4 %copy-start.1 = (f32[128,2048]{1,0:T(8,128)S(1)}, f32[128,2048]{1,0:T(8,128)}, u32[]{:S(2)}) copy-start(f32[128,2048]{1,0:T(8,128)} %emb_anchor.1) | copy-start | bytes 3145732
  4.2 104.4 %copy-start.2 = (f32[128,2048]{1,0:T(8,128)S(1)}, f32[128,2048]{1,0:T(8,128)}, u32[]{:S(2)}) copy-start(f32[128,2048]{1,0:T(8,128)} %param.15) | copy-start | bytes 3145732
  108.5 6.9 %copy-start = (f32[104,8,2048]{2,1,0:T(8,128)S(1)}, f32[104,8,2048]{2,1,0:T(8,128)}, u32[]{:S(2)}) copy-start(f32[104,8,2048]{2,1,0:T(8,128)} %get-tuple-element.28) | copy-start | bytes 20447236
